TPU v7x, 512 devices: a whole 4x4x16 slice. The times are simulated.
512 devices in a mesh: grp: 4 (over x), slab: 128 (over z, y, core).
Axes of the slice: x: 4, y: 4, z: 16, core: 2. Of those that a mesh axis runs over, the one named last changes fastest.
Arguments:
- margin: bfloat16 [2048, 5, 128, 128], P(('grp', 'slab')), may hold values from -2 to 2
- factor: bfloat16 [2048, 5, 128, 128], P(('grp', 'slab')), may hold values from -2 to 2
- pattern: int32 [2048, 5], P(('grp', 'slab')), may hold values from 0 to 1, as said below
Outputs:
- refined: bfloat16 [2048, 5, 128, 128], P(('grp', 'slab'))
- defect_norm: float32 [], replicated
Inputs may be any that keep to these rules, and one draw needn't show every extreme that they name: The pattern is symmetric: pattern[j, o] equals pattern[j + o - 2, 4 - o]. The diagonal block (o = 2) is always present and blocks whose row lies outside the matrix are absent; the share of present blocks varies from region to region.
All inputs are finite; a program needn't handle non-finite values.
Results may differ from a plain program's by a relative error of at most 0.0054.
Values may be sent and summed in bfloat16 or wider, within the bound.
A program may use at most 64 MiB of HBM per device.

v0:
```python
import jax
import jax.numpy as jnp
from jax import lax
from jax.sharding import PartitionSpec as P


def padded(cells, sides, width):
    for axis, dim in sides:
        count = lax.axis_size(axis)
        ends = count - 1
        head = lax.slice_in_dim(cells, 0, width, axis=dim)
        tail = lax.slice_in_dim(cells, cells.shape[dim] - width, cells.shape[dim], axis=dim)
        cells = jnp.concatenate(
            [
                lax.ppermute(tail, axis, [(i, (i + 1) % count) for i in range(ends)]),
                cells,
                lax.ppermute(head, axis, [((i + 1) % count, i) for i in range(ends)]),
            ],
            axis=dim,
        )
    return cells


def image_terms(band_half):
    return [
        [
            (inner_lag, outer_lag - inner_lag + band_half, inner_lag + band_half)
            for inner_lag in range(
                max(-band_half, outer_lag - band_half), min(band_half, outer_lag + band_half) + 1
            )
        ]
        for outer_lag in range(-2 * band_half, 2 * band_half + 1)
    ]


def defect_terms(band_half):
    return [
        [
            (outer_lag, inner_lag - outer_lag + band_half, inner_lag + 2 * band_half)
            for inner_lag in range(outer_lag - band_half, outer_lag + band_half + 1)
        ]
        for outer_lag in range(-band_half, band_half + 1)
    ]


def near_terms(band_half):
    return [
        [
            (inner_lag, outer_lag - inner_lag + band_half, inner_lag + band_half)
            for inner_lag in range(
                max(-band_half, outer_lag - band_half), min(band_half, outer_lag + band_half) + 1
            )
        ]
        for outer_lag in range(-band_half, band_half + 1)
    ]


def band_product(left_ext, right_own, term_list, transpose_left, band_half, columns):
    left_stack = jnp.stack(
        [
            left_ext[band_half + column_shift : band_half + column_shift + columns, left_offset]
            for column_shift, left_offset, right_offset in term_list
        ],
        axis=1,
    )
    right_stack = jnp.stack(
        [right_own[:, right_offset] for column_shift, left_offset, right_offset in term_list],
        axis=1,
    )
    einsum_form = "cbkm,cbkn->cmn" if transpose_left else "cbmk,cbkn->cmn"
    return jnp.einsum(einsum_form, left_stack, right_stack, preferred_element_type=jnp.float32)


def stack_offsets(left_ext, right_own, term_lists, transpose_left, band_half, columns):
    outputs = [
        band_product(left_ext, right_own, term_list, transpose_left, band_half, columns)
        for term_list in term_lists
    ]
    return jnp.stack(outputs, axis=1)


def defect_halo(defect, band_half):
    return padded(defect, ((("grp", "slab"), 0),), band_half)


def defect_measure(defect, columns, block_size):
    partial_sum = jnp.sum(jnp.square(defect.astype(jnp.float32)))
    squares_sum = lax.psum(partial_sum, ("grp", "slab"))
    entries = columns * lax.axis_size("grp") * lax.axis_size("slab") * block_size
    return jnp.sqrt(squares_sum / entries)


def per_device(margin, factor, pattern):
    columns = margin.shape[0]
    offsets = margin.shape[1]
    band_half = (offsets - 1) // 2
    block_size = margin.shape[2]
    present = pattern.astype(jnp.bfloat16)[:, :, None, None]
    mask_here = present.astype(jnp.float32)
    first_col = lax.axis_index(("grp", "slab")) * columns
    quarter_len = columns * lax.axis_size("slab")
    block_rows = (
        first_col
        + jnp.arange(columns, dtype=jnp.int32)[:, None]
        + jnp.arange(offsets, dtype=jnp.int32)[None, :]
        - band_half
    )
    in_quarter = (block_rows // quarter_len == lax.axis_index("grp")).astype(jnp.bfloat16)[
        :, :, None, None
    ]
    s_eff = margin * present
    z_eff = factor * present * in_quarter
    centre = (jnp.arange(offsets, dtype=jnp.int32) == band_half).astype(jnp.float32)[
        None, :, None, None
    ] * jnp.eye(block_size, dtype=jnp.float32)[None, None]
    joined = jnp.concatenate((s_eff, z_eff), axis=1)
    joined_ext = padded(joined, ((("grp", "slab"), 0),), band_half)
    s_ext = joined_ext[:, :offsets]
    z_ext = joined_ext[:, offsets:]
    applied = stack_offsets(s_ext, z_eff, image_terms(band_half), False, band_half, columns).astype(
        jnp.bfloat16
    )
    defect = (
        mask_here
        * (
            centre
            - stack_offsets(z_ext, applied, defect_terms(band_half), True, band_half, columns)
        )
    ).astype(jnp.bfloat16)
    defect_norm = defect_measure(defect, columns, block_size)
    d_ext = defect_halo(defect, band_half)
    square = (
        mask_here * stack_offsets(d_ext, defect, near_terms(band_half), False, band_half, columns)
    ).astype(jnp.bfloat16)
    first_part = stack_offsets(z_ext, defect, near_terms(band_half), False, band_half, columns)
    second_part = stack_offsets(z_ext, square, near_terms(band_half), False, band_half, columns)
    refined = (
        mask_here * (z_eff.astype(jnp.float32) + 0.5 * first_part + 0.375 * second_part)
    ).astype(jnp.bfloat16)
    return (refined, defect_norm)


def solution(mesh):
    return jax.shard_map(
        per_device,
        mesh=mesh,
        in_specs=(
            P(("grp", "slab"), None, None, None),
            P(("grp", "slab"), None, None, None),
            P(("grp", "slab"), None),
        ),
        out_specs=(P(("grp", "slab"), None, None, None), P()),
        check_vma=False,
    )
```

profile of v0, /device:TPU:1, one launch (start us, length us, event | category | flops | bytes accessed | tf_op | source)
XLA Modules:
  0.0 166.4 jit_solution(10530419525648659969)
XLA Ops:
  0.7 0.7 convert_element_type.44
  1.4 0.1 copy.6
  1.5 1.5 copy_multiply_fusion
  2.9 1.0 pad_maximum_fusion.1
  3.9 4.6 %collective-permute-start = (bf16[2,10,128,128]{3,2,0,1:T(8,128)(2,1)}, bf16[2,10,128,128]{3,2,0,1:T(8,128)(2,1)S(1)}, u32[]{:S(2)}, u32[]{:S(2)}) collective-permute-start(bf16[2,10,128,128]{3,2,0,1:T(8,128)(2,1)} %get-tuple-element.39), channel_id=1, source_target_pairs={{0,1},{1,2},{2,3},{3,4},{4,5},{5,6},{6,7},{7,8},{8,9},{9,10},{10,1... | collective-permute-start | bytes 1966088 | tf_op jit(solution)/shard_map/ppermute | solution.py:15
  8.5 5.5 %collective-permute-start.1 = (bf16[2,10,128,128]{3,2,0,1:T(8,128)(2,1)S(1)}, bf16[2,10,128,128]{3,2,0,1:T(8,128)(2,1)S(1)}, u32[]{:S(2)}, u32[]{:S(2)}) collective-permute-start(bf16[2,10,128,128]{3,2,0,1:T(8,128)(2,1)S(1)} %get-tuple-element.38), channel_id=1, source_target_pairs={{1,0},{2,1},{3,2},{4,3},{5,4},{6,5},{7,6},{8,7},{9,8},{10,9},{11,1... | collective-permute-start | bytes 1966088 | tf_op jit(solution)/shard_map/ppermute | solution.py:17
  14.0 0.1 copy.5
  14.1 0.1 broadcast_multiply_fusion
  14.2 2.1 %collective-permute-done = bf16[2,10,128,128]{3,2,0,1:T(8,128)(2,1)S(1)} collective-permute-done((bf16[2,10,128,128]{3,2,0,1:T(8,128)(2,1)}, bf16[2,10,128,128]{3,2,0,1:T(8,128)(2,1)S(1)}, u32[]{:S(2)}, u32[]{:S(2)}) %collective-permute-start) | collective-permute-done | bytes 655392 | tf_op jit(solution)/shard_map/ppermute | solution.py:15
  16.3 4.1 %collective-permute-done.1 = bf16[2,10,128,128]{3,2,0,1:T(8,128)(2,1)S(1)} collective-permute-done((bf16[2,10,128,128]{3,2,0,1:T(8,128)(2,1)S(1)}, bf16[2,10,128,128]{3,2,0,1:T(8,128)(2,1)S(1)}, u32[]{:S(2)}, u32[]{:S(2)}) %collective-permute-start.1) | collective-permute-done | bytes 655392 | tf_op jit(solution)/shard_map/ppermute | solution.py:17
  20.4 0.4 pad_maximum_fusion
  20.8 0.2 fusion.34
  21.0 0.3 fusion.211
  21.4 0.7 fusion.212
  22.2 1.0 fusion.210
  23.1 0.2 constant_dynamic-update-slice_fusion.8
  23.4 0.3 constant_dynamic-update-slice_fusion.13
  23.7 0.4 constant_dynamic-update-slice_fusion.18
  24.0 0.4 constant_dynamic-update-slice_fusion.22
  24.5 0.4 constant_dynamic-update-slice_fusion.21
  24.9 0.3 constant_dynamic-update-slice_fusion.20
  25.2 0.3 constant_dynamic-update-slice_fusion.19
  25.5 0.2 fusion.36
  25.7 0.4 fusion.3
  26.1 0.4 fusion.2
  26.5 0.4 fusion.19
  26.9 0.4 fusion.1
  27.3 0.4 fusion
  27.7 1.2 multiply_reduce_fusion
  28.9 0.9 fusion.214
  29.8 1.9 %collective-permute-start.2 = (bf16[2,5,128,128]{3,2,0,1:T(8,128)(2,1)}, bf16[2,5,128,128]{3,2,0,1:T(8,128)(2,1)}, u32[]{:S(2)}, u32[]{:S(2)}) collective-permute-start(bf16[2,5,128,128]{3,2,0,1:T(8,128)(2,1)} %get-tuple-element.51), channel_id=1, source_target_pairs={{0,1},{1,2},{2,3},{3,4},{4,5},{5,6},{6,7},{7,8},{8,9},{9,10},{10,1... | collective-permute-start | bytes 983048 | tf_op jit(solution)/shard_map/ppermute | solution.py:15
  31.7 3.1 %collective-permute-start.3 = (bf16[2,5,128,128]{3,2,0,1:T(8,128)(2,1)}, bf16[2,5,128,128]{3,2,0,1:T(8,128)(2,1)}, u32[]{:S(2)}, u32[]{:S(2)}) collective-permute-start(bf16[2,5,128,128]{3,2,0,1:T(8,128)(2,1)} %get-tuple-element.50), channel_id=1, source_target_pairs={{1,0},{2,1},{3,2},{4,3},{5,4},{6,5},{7,6},{8,7},{9,8},{10,9},{11,1... | collective-permute-start | bytes 983048 | tf_op jit(solution)/shard_map/ppermute | solution.py:17
  34.8 0.3 fusion.15
  35.2 0.3 fusion.14
  35.5 0.3 fusion.18
  35.8 0.3 fusion.13
  36.1 112.4 %psum.7 = f32[]{:T(128)} all-reduce(f32[]{:T(128)} %get-tuple-element.4), channel_id=1, replica_groups=mesh['grp'=4,'slab'=128] {'grp','slab'}, use_global_device_ids=true, to_apply=%region_1.2 | all-reduce | flops 1 | bytes 8 | tf_op jit(solution)/shard_map/psum | solution.py:88
  149.2 1.3 fusion.12
  150.5 0.9 fusion.213
  151.4 0.8 maximum_dynamic-update-slice_fusion.2
  152.2 0.8 maximum_dynamic-update-slice_fusion.1
  153.0 0.9 maximum_dynamic-update-slice_fusion
  153.9 1.3 fusion.11
  155.1 1.3 fusion.10
  156.4 0.3 fusion.17
  156.8 1.3 fusion.9
  158.0 1.3 fusion.8
  159.3 0.2 multiply_convert_fusion.1
  159.5 0.7 copy-done.3
  160.2 0.1 copy-done.5
  160.3 0.1 copy-done.12
  160.3 0.3 fusion.7
  160.6 0.6 copy-done.1
  161.4 0.3 fusion.6
  161.7 0.3 fusion.16
  162.0 0.5 copy-done.8
  162.6 0.1 copy-done.16
  162.6 0.1 copy-done.18
  162.7 0.3 fusion.5
  163.0 0.6 copy-done.6
  163.6 0.1 copy-done.13
  163.7 0.3 fusion.4
  164.0 0.4 multiply_convert_fusion
  164.4 0.9 copy.63
  (43 shorter events, 0.4 us)
Async XLA Ops:
  3.9 12.4 %collective-permute-start = (bf16[2,10,128,128]{3,2,0,1:T(8,128)(2,1)}, bf16[2,10,128,128]{3,2,0,1:T(8,128)(2,1)S(1)}, u32[]{:S(2)}, u32[]{:S(2)}) collective-permute-start(bf16[2,10,128,128]{3,2,0,1:T(8,128)(2,1)} %get-tuple-element.39), channel_id=1, source_target_pairs={{0,1},{1,2},{2,3},{3,4},{4,5},{5,6},{6,7},{7,8},{8,9},{9,10},{10,1... | collective-permute-start | bytes 1966088 | tf_op jit(solution)/shard_map/ppermute | solution.py:15
  8.5 11.9 %collective-permute-start.1 = (bf16[2,10,128,128]{3,2,0,1:T(8,128)(2,1)S(1)}, bf16[2,10,128,128]{3,2,0,1:T(8,128)(2,1)S(1)}, u32[]{:S(2)}, u32[]{:S(2)}) collective-permute-start(bf16[2,10,128,128]{3,2,0,1:T(8,128)(2,1)S(1)} %get-tuple-element.38), channel_id=1, source_target_pairs={{1,0},{2,1},{3,2},{4,3},{5,4},{6,5},{7,6},{8,7},{9,8},{10,9},{11,1... | collective-permute-start | bytes 1966088 | tf_op jit(solution)/shard_map/ppermute | solution.py:17
  21.3 13.5 %copy-start.2 = (bf16[4,1,128,128]{3,2,0,1:T(8,128)(2,1)}, bf16[4,1,128,128]{3,2,0,1:T(8,128)(2,1)S(1)}, u32[]{:S(2)}) copy-start(bf16[4,1,128,128]{3,2,0,1:T(8,128)(2,1)S(1)} %get-tuple-element.32) | copy-start | bytes 393220
  21.3 13.5 %copy-start.4 = (bf16[4,1,128,128]{3,2,0,1:T(8,128)(2,1)}, bf16[4,1,128,128]{3,2,0,1:T(8,128)(2,1)S(1)}, u32[]{:S(2)}) copy-start(bf16[4,1,128,128]{3,2,0,1:T(8,128)(2,1)S(1)} %get-tuple-element.33) | copy-start | bytes 393220
  21.3 13.8 %copy-start = (bf16[4,1,128,128]{3,2,0,1:T(8,128)(2,1)}, bf16[4,1,128,128]{3,2,0,1:T(8,128)(2,1)S(1)}, u32[]{:S(2)}) copy-start(bf16[4,1,128,128]{3,2,0,1:T(8,128)(2,1)S(1)} %get-tuple-element.23) | copy-start | bytes 393220
  22.1 12.7 %copy-start.11 = (bf16[4,1,128,128]{3,2,0,1:T(8,128)(2,1)}, bf16[4,1,128,128]{3,2,0,1:T(8,128)(2,1)S(1)}, u32[]{:S(2)}) copy-start(bf16[4,1,128,128]{3,2,0,1:T(8,128)(2,1)S(1)} %get-tuple-element.44) | copy-start | bytes 393220
  22.1 13.0 %copy-start.9 = (bf16[4,1,128,128]{3,2,0,1:T(8,128)(2,1)}, bf16[4,1,128,128]{3,2,0,1:T(8,128)(2,1)S(1)}, u32[]{:S(2)}) copy-start(bf16[4,1,128,128]{3,2,0,1:T(8,128)(2,1)S(1)} %get-tuple-element.43) | copy-start | bytes 393220
  22.1 13.7 %copy-start.7 = (bf16[4,1,128,128]{3,2,0,1:T(8,128)(2,1)}, bf16[4,1,128,128]{3,2,0,1:T(8,128)(2,1)S(1)}, u32[]{:S(2)}) copy-start(bf16[4,1,128,128]{3,2,0,1:T(8,128)(2,1)S(1)} %get-tuple-element.41) | copy-start | bytes 393220
  23.1 12.0 %copy-start.19 = (bf16[4,1,128,128]{3,2,0,1:T(8,128)(2,1)}, bf16[4,1,128,128]{3,2,0,1:T(8,128)(2,1)S(1)}, u32[]{:S(2)}) copy-start(bf16[4,1,128,128]{3,2,0,1:T(8,128)(2,1)S(1)} %get-tuple-element.10) | copy-start | bytes 393220
  23.1 12.7 %copy-start.15 = (bf16[4,1,128,128]{3,2,0,1:T(8,128)(2,1)}, bf16[4,1,128,128]{3,2,0,1:T(8,128)(2,1)S(1)}, u32[]{:S(2)}) copy-start(bf16[4,1,128,128]{3,2,0,1:T(8,128)(2,1)S(1)} %get-tuple-element.7) | copy-start | bytes 393220
  23.1 12.7 %copy-start.17 = (bf16[4,1,128,128]{3,2,0,1:T(8,128)(2,1)}, bf16[4,1,128,128]{3,2,0,1:T(8,128)(2,1)S(1)}, u32[]{:S(2)}) copy-start(bf16[4,1,128,128]{3,2,0,1:T(8,128)(2,1)S(1)} %get-tuple-element.8) | copy-start | bytes 393220
  29.8 120.7 %collective-permute-start.2 = (bf16[2,5,128,128]{3,2,0,1:T(8,128)(2,1)}, bf16[2,5,128,128]{3,2,0,1:T(8,128)(2,1)}, u32[]{:S(2)}, u32[]{:S(2)}) collective-permute-start(bf16[2,5,128,128]{3,2,0,1:T(8,128)(2,1)} %get-tuple-element.51), channel_id=1, source_target_pairs={{0,1},{1,2},{2,3},{3,4},{4,5},{5,6},{6,7},{7,8},{8,9},{9,10},{10,1... | collective-permute-start | bytes 983048 | tf_op jit(solution)/shard_map/ppermute | solution.py:15
  31.7 120.5 %collective-permute-start.3 = (bf16[2,5,128,128]{3,2,0,1:T(8,128)(2,1)}, bf16[2,5,128,128]{3,2,0,1:T(8,128)(2,1)}, u32[]{:S(2)}, u32[]{:S(2)}) collective-permute-start(bf16[2,5,128,128]{3,2,0,1:T(8,128)(2,1)} %get-tuple-element.50), channel_id=1, source_target_pairs={{1,0},{2,1},{3,2},{4,3},{5,4},{6,5},{7,6},{8,7},{9,8},{10,9},{11,1... | collective-permute-start | bytes 983048 | tf_op jit(solution)/shard_map/ppermute | solution.py:17
  159.3 0.9 copy-start.3
  159.3 1.0 copy-start.5
  159.3 1.0 copy-start.12
  160.3 0.9 copy-start.1
  160.3 1.0 copy-start.10
  160.3 1.0 copy-start.20
  161.7 0.9 copy-start.8
  161.7 1.0 copy-start.16
  161.7 1.0 copy-start.18
  162.7 0.9 copy-start.6
  162.7 1.0 copy-start.13
  162.7 1.0 copy-start.14
where the time goes:
time: 167 us; the launch traced here: 166 us
  blocking collectives  112 us (67%)
  starting transfers between devices  15.1 us (9%)
  matrix products  13.9 us (8%)
  other arithmetic  8.69 us (5%)
  local copies, waits for them, and re-layouts  7.08 us (4%)
  waiting for transfers between devices  6.19 us (4%)
  between operations  2.96 us (2%)
    psum x1, blocking collectives, defect_measure(): squares_sum = lax.psum(partial_sum, ('grp', 'slab'))  112 us
    dot_general x29, matrix products, band_product(): jnp.einsum(einsum_form, left_stack, right_stack, preferred_element_type=j...  13.9 us
    ppermute x2, starting transfers between devices, padded(): lax.ppermute(head, axis, [((i + 1) % count, i) for i in range(ends)])  8.63 us
    ppermute x2, starting transfers between devices, padded(): lax.ppermute(tail, axis, [(i, (i + 1) % count) for i in range(ends)])  6.48 us
    ppermute x2, waiting for transfers between devices, padded(): lax.ppermute(head, axis, [((i + 1) % count, i) for i in range(ends)])  4.08 us
    unnamed x47, local copies, waits for them, and re-layouts  4.01 us
  transfers between devices with their start and end apart: 4, of which 2 were waited for; matrix products, arithmetic and copies ran while one was open for 3% of the time, Pallas kernels for 0%

commit v1 on v0

v1 whole, which is shorter than its diff:
```python
import functools

import jax
import jax.numpy as jnp
from jax import lax
from jax.experimental import pallas as pl
from jax.experimental.pallas import tpu as pltpu
from jax.sharding import PartitionSpec as P

B = 128
W = 2
OFFS = 2 * W + 1
COLS = 4
SUP = 2 * B
BAND = 3 * SUP
PLANE = 8
MESH = pl.DeviceIdType.MESH


def dot(left, right):
    return jnp.dot(left, right, preferred_element_type=jnp.float32)


def kernel(
    n_grp,
    n_slab,
    margin,
    factor,
    pat,
    out,
    norm,
    sb,
    zb,
    zt,
    pb,
    db,
    eb,
    tu,
    td,
    ts,
    acc,
    acc2,
    part_a,
    part_b,
    load_sem,
    send_sem,
    recv_sem,
    sum_send,
    sum_recv,
):
    grp = lax.axis_index("grp")
    slab = lax.axis_index("slab")
    count = n_grp * n_slab
    n_plane = n_grp * PLANE
    n_z = n_slab // PLANE
    here = grp * n_slab + slab

    def device(flat):
        return (lax.div(flat, n_slab), lax.rem(flat, n_slab))

    right = device(lax.rem(here + 1, count))
    left = device(lax.rem(here + count - 1, count))
    z_here = lax.div(slab, PLANE)
    in_plane = grp * PLANE + lax.rem(slab, PLANE)

    def plane_device(index):
        return (lax.div(index, PLANE), z_here * PLANE + lax.rem(index, PLANE))

    def z_device(index):
        return (grp, index * PLANE + lax.rem(slab, PLANE))

    loads = []
    for column in (0, 3, 1, 2):
        for which, (source, band) in enumerate(((margin, sb), (factor, zb))):
            half = column % 2
            copy = pltpu.make_async_copy(
                source.at[column],
                band.at[1 + column // 2, pl.ds(half * B, OFFS * B), pl.ds(half * B, B)],
                load_sem.at[2 * column + which],
            )
            copy.start()
            loads.append((column, which, copy))

    barrier = pltpu.get_barrier_semaphore()
    for neighbour in (left, right):
        pl.semaphore_signal(barrier, inc=1, device_id=neighbour, device_id_type=MESH)

    def greet_plane(step, carry):
        peer = plane_device(lax.rem(in_plane + step, n_plane))
        pl.semaphore_signal(barrier, inc=1, device_id=peer, device_id_type=MESH)
        return carry

    def greet_z(step, carry):
        peer = z_device(lax.rem(z_here + step, n_z))
        pl.semaphore_signal(barrier, inc=1, device_id=peer, device_id_type=MESH)
        return carry

    lax.fori_loop(1, n_z, greet_z, 0)
    lax.fori_loop(1, n_plane, greet_plane, 0)

    blank = jnp.zeros((B, B), jnp.bfloat16)
    for band in (sb, zb, db):
        for index in range(4):
            band[index, pl.ds(5 * B, B), pl.ds(0, B)] = blank
            band[index, pl.ds(0, B), pl.ds(B, B)] = blank
    for index in range(2):
        eb[index, pl.ds(5 * B, B), pl.ds(0, B)] = blank
        eb[index, pl.ds(0, B), pl.ds(B, B)] = blank

    def present(column, offset):
        return pat[column, offset].astype(jnp.float32)

    first = (slab > 0).astype(jnp.float32)
    last = (slab < n_slab - 1).astype(jnp.float32)

    for column, which, copy in loads:
        copy.wait()
        half = column % 2
        band = (sb, zb)[which]
        for offset in range(OFFS):
            scale = present(column, offset)
            row = column + offset - W
            if which == 1 and row < 0:
                scale = scale * first
            if which == 1 and row >= COLS:
                scale = scale * last
            where = (1 + column // 2, pl.ds((half + offset) * B, B), pl.ds(half * B, B))
            band[where] = (band[where].astype(jnp.float32) * scale).astype(jnp.bfloat16)

    pl.semaphore_wait(barrier, 2 + (n_plane - 1) + (n_z - 1))

    started = []

    def send(source, target, peer):
        index = len(started)
        copy = pltpu.make_async_remote_copy(
            src_ref=source,
            dst_ref=target,
            send_sem=send_sem.at[index],
            recv_sem=recv_sem.at[index],
            device_id=peer,
            device_id_type=MESH,
        )
        copy.start()
        started.append(copy)
        return copy

    def send_band(band):
        to_left = [
            send(
                band.at[1, pl.ds(first_row, rows), pl.ds(half * B, B)],
                band.at[3, pl.ds(first_row, rows), pl.ds(half * B, B)],
                left,
            )
            for half, first_row, rows in ((0, 0, 4 * B), (1, B, 3 * B))
        ]
        to_right = [
            send(
                band.at[2, pl.ds(first_row, rows), pl.ds(half * B, B)],
                band.at[0, pl.ds(first_row, rows), pl.ds(half * B, B)],
                right,
            )
            for half, first_row, rows in ((0, 2 * B, 3 * B), (1, 2 * B, 4 * B))
        ]
        return to_left + to_right

    s_halo = send_band(sb)
    z_halo = send_band(zb)

    def flip(inner, outer):
        value = zb[outer + 1, pl.ds((inner - outer + 1) * SUP, SUP), :]
        zt[inner + 1, pl.ds((outer - inner + 1) * SUP, SUP), :] = value.T

    for outer in (0, 1):
        for inner in (outer - 1, outer, outer + 1):
            flip(inner, outer)

    def upper(column):
        return dot(zt[column, pl.ds(2 * SUP, SUP), :], sb[column + 1, pl.ds(0, SUP), :])

    def lower(column):
        return dot(zt[column + 2, pl.ds(0, SUP), :], sb[column + 1, pl.ds(2 * SUP, SUP), :])

    ts[0] = lower(0).astype(jnp.bfloat16)
    ts[1] = upper(1).astype(jnp.bfloat16)
    t_halo = [send(ts.at[0], td.at[1], left), send(ts.at[1], tu.at[0], right)]
    tu[1] = upper(0).astype(jnp.bfloat16)
    td[0] = lower(1).astype(jnp.bfloat16)

    def near(bands, values, own, row, inners):
        total = None
        for inner in inners:
            if abs(row - inner) > 1:
                continue
            term = dot(
                bands[own + inner, pl.ds((row - inner + 1) * SUP, SUP), :],
                values[pl.ds(inner * SUP, SUP), :],
            )
            total = term if total is None else total + term
        return total

    local = {0: (1, 2), 1: (0, 1)}
    halo = {0: 0, 1: 2}

    for own in (0, 1):
        for row in range(3):
            acc[own, pl.ds(row * SUP, SUP), :] = near(sb, zb.at[own + 1], own, row, local[own])

    for copy in s_halo:
        copy.wait_recv()
    for own in (0, 1):
        for row in range(3):
            where = (own, pl.ds(row * SUP, SUP), slice(None))
            total = acc[where]
            extra = near(sb, zb.at[own + 1], own, row, (halo[own],))
            if extra is not None:
                total = total + extra
            pb[where] = total.astype(jnp.bfloat16)

    eye = (
        lax.broadcasted_iota(jnp.int32, (B, B), 0) == lax.broadcasted_iota(jnp.int32, (B, B), 1)
    ).astype(jnp.float32)

    def blocks_of(own, row):
        for r in range(2):
            for c in range(2):
                offset = 2 * row + r - c
                if 0 <= offset < OFFS:
                    yield r, c, 2 * own + c, offset

    squares = jnp.zeros((8, B), jnp.float32)

    def defect(own, row, squares):
        total = near(zt, pb.at[own], own, row, (0, 1, 2))
        if row == 0:
            total = total + dot(tu[own], zb[own + 1, pl.ds(0, SUP), :])
        if row == 2:
            total = total + dot(td[own], zb[own + 1, pl.ds(2 * SUP, SUP), :])
        for r, c, column, offset in blocks_of(own, row):
            block = -total[r * B : (r + 1) * B, c * B : (c + 1) * B]
            if offset == W:
                block = eye + block
            block = (block * present(column, offset)).astype(jnp.bfloat16)
            db[own + 1, pl.ds((2 * row + r) * B, B), pl.ds(c * B, B)] = block
            wide = block.astype(jnp.float32)
            squares = squares + jnp.sum((wide * wide).reshape(B // 8, 8, B), axis=0)
        return squares

    for own, rows in ((0, (1, 2)), (1, (0, 1))):
        for row in rows:
            squares = defect(own, row, squares)

    for copy in z_halo + t_halo:
        copy.wait_recv()
    flip(-1, -1)
    flip(0, -1)
    flip(1, 2)
    flip(2, 2)
    squares = defect(0, 0, squares)
    squares = defect(1, 2, squares)

    d_halo = send_band(db)

    part_a[in_plane] = jnp.sum(squares, axis=0, keepdims=True)

    def sum_copy(buffer, slot, stage, peer):
        return pltpu.make_async_remote_copy(
            src_ref=buffer.at[slot],
            dst_ref=buffer.at[slot],
            send_sem=sum_send.at[stage],
            recv_sem=sum_recv.at[stage],
            device_id=peer,
            device_id_type=MESH,
        )

    def send_plane(step, carry):
        sum_copy(part_a, in_plane, 0, plane_device(lax.rem(in_plane + step, n_plane))).start()
        return carry

    def send_z(step, carry):
        sum_copy(part_b, z_here, 1, z_device(lax.rem(z_here + step, n_z))).start()
        return carry

    def all_of(buffer, rows, sem):
        return pltpu.make_async_copy(buffer.at[pl.ds(0, rows)], buffer.at[pl.ds(0, rows)], sem)

    lax.fori_loop(1, n_plane, send_plane, 0)

    for own in (0, 1):
        for row in range(3):
            where = (own, pl.ds(row * SUP, SUP), slice(None))
            acc[where] = near(zb, db.at[own + 1], own, row, (0, 1, 2))
            acc2[where] = near(db, db.at[own + 1], own, row, local[own])

    all_of(part_a, n_plane - 1, sum_recv.at[0]).wait()
    part_b[z_here] = jnp.sum(part_a[...], axis=0)
    lax.fori_loop(1, n_z, send_z, 0)

    for copy in d_halo:
        copy.wait_recv()
    for own in (0, 1):
        for row in range(3):
            total = acc2[own, pl.ds(row * SUP, SUP), :]
            extra = near(db, db.at[own + 1], own, row, (halo[own],))
            if extra is not None:
                total = total + extra
            for r, c, column, offset in blocks_of(own, row):
                block = total[r * B : (r + 1) * B, c * B : (c + 1) * B]
                block = (block * present(column, offset)).astype(jnp.bfloat16)
                eb[own, pl.ds((2 * row + r) * B, B), pl.ds(c * B, B)] = block

    for own in (0, 1):
        for row in range(3):
            total = 0.375 * near(zb, eb.at[own], own, row, (0, 1, 2))
            total = total + 0.5 * acc[own, pl.ds(row * SUP, SUP), :]
            for r, c, column, offset in blocks_of(own, row):
                block = total[r * B : (r + 1) * B, c * B : (c + 1) * B]
                base = zb[own + 1, pl.ds((2 * row + r) * B, B), pl.ds(c * B, B)]
                block = (block + base.astype(jnp.float32)) * present(column, offset)
                out[column, offset] = block.astype(jnp.bfloat16)

    all_of(part_b, n_z - 1, sum_recv.at[1]).wait()
    total = jnp.sum(jnp.sum(part_b[...], axis=0), axis=1, keepdims=True)
    norm[...] = jnp.sqrt(total / (count * COLS * B))

    for copy in started:
        copy.wait_send()
    all_of(part_a, n_plane - 1, sum_send.at[0]).wait()
    all_of(part_b, n_z - 1, sum_send.at[1]).wait()


def solution(mesh):
    n_grp, n_slab = mesh.shape["grp"], mesh.shape["slab"]
    n_plane, n_z = n_grp * PLANE, n_slab // PLANE

    def step(margin, factor, pattern):
        bands = pltpu.VMEM((4, BAND, SUP), jnp.bfloat16)
        pairs = pltpu.VMEM((2, BAND, SUP), jnp.bfloat16)
        wide = pltpu.VMEM((2, BAND, SUP), jnp.float32)
        corner = pltpu.VMEM((2, SUP, SUP), jnp.bfloat16)
        refined, norm = pl.pallas_call(
            functools.partial(kernel, n_grp, n_slab),
            out_shape=(
                jax.ShapeDtypeStruct((COLS, OFFS, B, B), jnp.bfloat16),
                jax.ShapeDtypeStruct((1, 1), jnp.float32),
            ),
            in_specs=[
                pl.BlockSpec(memory_space=pl.ANY),
                pl.BlockSpec(memory_space=pl.ANY),
                pl.BlockSpec(memory_space=pltpu.SMEM),
            ],
            out_specs=(
                pl.BlockSpec(memory_space=pltpu.VMEM),
                pl.BlockSpec(memory_space=pltpu.VMEM),
            ),
            scratch_shapes=[
                bands,
                bands,
                bands,
                pairs,
                bands,
                pairs,
                corner,
                corner,
                corner,
                wide,
                wide,
                pltpu.VMEM((n_plane, 1, B), jnp.float32),
                pltpu.VMEM((n_z, 1, B), jnp.float32),
                pltpu.SemaphoreType.DMA((2 * COLS,)),
                pltpu.SemaphoreType.DMA((14,)),
                pltpu.SemaphoreType.DMA((14,)),
                pltpu.SemaphoreType.DMA((2,)),
                pltpu.SemaphoreType.DMA((2,)),
            ],
            compiler_params=pltpu.CompilerParams(collective_id=0, has_side_effects=True),
        )(
            margin.reshape(COLS, OFFS * B, B),
            factor.reshape(COLS, OFFS * B, B),
            pattern,
        )
        return refined, norm.reshape(())

    return jax.shard_map(
        step,
        mesh=mesh,
        in_specs=(
            P(("grp", "slab"), None, None, None),
            P(("grp", "slab"), None, None, None),
            P(("grp", "slab"), None),
        ),
        out_specs=(P(("grp", "slab"), None, None, None), P()),
        check_vma=False,
    )
```

time: 167 us -> 44.1 us (0.26)
  blocking collectives: 112 us -> 0 us
  Pallas kernels: 0 us -> 39.5 us
  starting transfers between devices: 15.1 us -> 0 us
  matrix products: 13.9 us -> 0 us
  other arithmetic: 8.69 us -> 0 us
  waiting for transfers between devices: 6.19 us -> 0 us
  local copies, waits for them, and re-layouts: 7.08 us -> 1.99 us
    psum x1 -> x0, blocking collectives: 112 us -> none  [defect_measure(): squares_sum = lax.psum(partial_sum, ('grp', 'slab'))]
    pallas_call x0 -> x1, Pallas kernels: none -> 39.5 us  [step(): pl.pallas_call(functools.partial(kernel, n_grp, n_slab), out_shape=(jax.S...]
    ppermute x4 -> x0, starting transfers between devices: 15.1 us -> none  [the longest x2 8.63 us: padded(): lax.ppermute(head, axis, [((i + 1) % count, i) for i in range(ends)])]
    dot_general x29 -> x0, matrix products: 13.9 us -> none  [band_product(): jnp.einsum(einsum_form, left_stack, right_stack, preferred_element_type=j...]
    ppermute x4 -> x0, waiting for transfers between devices: 6.19 us -> none  [the longest x2 4.08 us: padded(): lax.ppermute(head, axis, [((i + 1) % count, i) for i in range(ends)])]
    slice x4 -> x0, local copies, waits for them, and re-layouts: 2.86 us -> none  [the longest x2 1.23 us: band_product(): left_ext[band_half + column_shift:band_half + column_shift + columns, lef...]
    unnamed x47 -> x1, local copies, waits for them, and re-layouts: 4.01 us -> 1.99 us
  transfers between devices with their start and end apart: 4 -> 0, of which waited for: 2 -> 0; matrix products, arithmetic and copies ran while one was open for 3% -> 0% of each run, Pallas kernels for 0% -> 0%
where the time goes in v1:
time: 44.1 us; the launch traced here: 43.8 us
  Pallas kernels  39.5 us (90%)
  between operations  2.39 us (5%)
  local copies, waits for them, and re-layouts  1.99 us (5%)
    pallas_call x1, Pallas kernels, step(): pl.pallas_call(functools.partial(kernel, n_grp, n_slab), out_shape=(jax.S...  39.5 us
    unnamed x1, local copies, waits for them, and re-layouts  1.99 us

profile of v1, /device:TPU:1, one launch (start us, length us, event | category | flops | bytes accessed | tf_op | source)
XLA Modules:
  0.0 43.8 jit_solution(2235095707181755617)
XLA Ops:
  0.6 39.5 %shard_map.50 = (bf16[4,5,128,128]{3,2,1,0:T(8,128)(2,1)}, f32[1,1]{1,0:T(1,128)}) custom-call(bf16[4,640,128]{2,1,0:T(8,128)(2,1)} %bitcast.3, bf16[4,640,128]{2,1,0:T(8,128)(2,1)} %bitcast.4, s32[4,5]{1,0:T(4,128)} %pat.1), custom_call_target="tpu_custom_call" | custom-call | tf_op jit(solution)/shard_map/pallas_call | solution.py:341
  40.1 2.0 %copy.7 = bf16[4,5,128,128]{3,2,1,0:T(8,128)(2,1)} copy(bf16[4,5,128,128]{3,2,1,0:T(8,128)(2,1)} %get-tuple-element.8) | data formatting | bytes 1310720

commit v2 on v1

--- a/solution.py
+++ b/solution.py
@@ -14,6 +14,7 @@
 SUP = 2 * B
 BAND = 3 * SUP
 PLANE = 8
+COPIES = 26
 MESH = pl.DeviceIdType.MESH
 
 
@@ -47,6 +48,7 @@
     recv_sem,
     sum_send,
     sum_recv,
+    known,
 ):
     grp = lax.axis_index("grp")
     slab = lax.axis_index("slab")
@@ -69,9 +71,9 @@
     def z_device(index):
         return (grp, index * PLANE + lax.rem(slab, PLANE))
 
-    loads = []
-    for column in (0, 3, 1, 2):
-        for which, (source, band) in enumerate(((margin, sb), (factor, zb))):
+    loads = {}
+    for which, (source, band) in enumerate(((margin, sb), (factor, zb))):
+        for column in range(COLS):
             half = column % 2
             copy = pltpu.make_async_copy(
                 source.at[column],
@@ -79,24 +81,29 @@
                 load_sem.at[2 * column + which],
             )
             copy.start()
-            loads.append((column, which, copy))
+            loads[which, column] = copy
+
+    row_here, core = lax.div(lax.rem(slab, PLANE), 2), lax.rem(slab, 2)
+    n_row = PLANE // 2
+
+    def along_x(step):
+        return (lax.rem(grp + n_grp + step, n_grp), slab)
+
+    def along_y(step):
+        return (grp, z_here * PLANE + lax.rem(row_here + n_row + step, n_row) * 2 + core)
+
+    def along_z(step):
+        return (grp, lax.rem(slab + n_slab + step * PLANE, n_slab))
+
+    mate = (grp, slab + 1 - 2 * core)
+
+    def signal(sem, *peers):
+        for peer in peers:
+            pl.semaphore_signal(sem, inc=1, device_id=peer, device_id_type=MESH)
 
     barrier = pltpu.get_barrier_semaphore()
-    for neighbour in (left, right):
-        pl.semaphore_signal(barrier, inc=1, device_id=neighbour, device_id_type=MESH)
-
-    def greet_plane(step, carry):
-        peer = plane_device(lax.rem(in_plane + step, n_plane))
-        pl.semaphore_signal(barrier, inc=1, device_id=peer, device_id_type=MESH)
-        return carry
-
-    def greet_z(step, carry):
-        peer = z_device(lax.rem(z_here + step, n_z))
-        pl.semaphore_signal(barrier, inc=1, device_id=peer, device_id_type=MESH)
-        return carry
-
-    lax.fori_loop(1, n_z, greet_z, 0)
-    lax.fori_loop(1, n_plane, greet_plane, 0)
+    near_by = (left, right, along_y(1), along_y(-1), along_x(1), along_x(-1), along_z(1), along_z(-1))
+    signal(barrier, *near_by)
 
     blank = jnp.zeros((B, B), jnp.bfloat16)
     for band in (sb, zb, db):
@@ -113,21 +120,14 @@
     first = (slab > 0).astype(jnp.float32)
     last = (slab < n_slab - 1).astype(jnp.float32)
 
-    for column, which, copy in loads:
-        copy.wait()
-        half = column % 2
-        band = (sb, zb)[which]
-        for offset in range(OFFS):
-            scale = present(column, offset)
-            row = column + offset - W
-            if which == 1 and row < 0:
-                scale = scale * first
-            if which == 1 and row >= COLS:
-                scale = scale * last
-            where = (1 + column // 2, pl.ds((half + offset) * B, B), pl.ds(half * B, B))
-            band[where] = (band[where].astype(jnp.float32) * scale).astype(jnp.bfloat16)
-
-    pl.semaphore_wait(barrier, 2 + (n_plane - 1) + (n_z - 1))
+    def place(index, half, block, blocks=1):
+        return (index, pl.ds(block * B, blocks * B), pl.ds(half * B, B))
+
+    def scale_block(band, where, scale):
+        factors = jnp.full((B, B), scale, jnp.float32).astype(jnp.bfloat16)
+        band[where] = band[where] * factors
+
+    pl.semaphore_wait(barrier, len(near_by))
 
     started = []
 
@@ -164,8 +164,71 @@
         ]
         return to_left + to_right
 
-    s_halo = send_band(sb)
-    z_halo = send_band(zb)
+    raw_left, raw_right = ((0, 0, 3), (1, 0, 1), (1, 2, 1)), ((2, 2, 1), (2, 4, 1), (3, 2, 3))
+    own_left, own_right = ((0, 3), (1, 1)), ((2, 3), (3, 1))
+
+    def send_raw(source, band):
+        copies = []
+        for index in range(3):
+            for peer, target, pieces in ((left, 3, raw_left), (right, 0, raw_right)):
+                column, offset, offsets = pieces[index]
+                half = column % 2
+                copies.append(
+                    send(
+                        source.at[column, pl.ds(offset * B, offsets * B), :],
+                        band.at[place(target, half, offset + half, offsets)],
+                        peer,
+                    )
+                )
+        return copies
+
+    def send_own(band):
+        copies = []
+        for index in range(2):
+            for peer, target, pieces in ((left, 3, own_left), (right, 0, own_right)):
+                column, offset = pieces[index]
+                half = column % 2
+                copies.append(
+                    send(
+                        band.at[place(1 + column // 2, half, offset + half)],
+                        band.at[place(target, half, offset + half)],
+                        peer,
+                    )
+                )
+        return copies
+
+    s_halo = send_raw(margin, sb)
+    z_halo = send_raw(factor, zb)
+    signal(known.at[0], along_y(1), along_y(-1))
+    signal(known.at[3], along_z(1), along_z(-1))
+
+    for which, (band, halo_copies) in enumerate(((sb, s_halo), (zb, z_halo))):
+        for column in range(COLS):
+            loads[which, column].wait()
+        for column in range(COLS):
+            half = column % 2
+            for offset in range(OFFS):
+                if offset == W:
+                    continue
+                scale = present(column, offset)
+                row = column + offset - W
+                if which == 1 and row < 0:
+                    scale = scale * first
+                if which == 1 and row >= COLS:
+                    scale = scale * last
+                scale_block(band, place(1 + column // 2, half, half + offset), scale)
+        halo_copies.extend(send_own(band))
+
+    def mask_halo(band, low, high):
+        for half, block, column, offset in ((0, 4, 0, 0), (1, 4, 0, 1), (1, 5, 1, 0)):
+            scale_block(band, place(0, half, block), present(column, offset) * low)
+        for half, block, column, offset in ((0, 0, 2, 4), (0, 1, 3, 3), (1, 1, 3, 4)):
+            scale_block(band, place(3, half, block), present(column, offset) * high)
+
+    pl.semaphore_wait(known.at[0], 2)
+    signal(known.at[1], mate)
+    pl.semaphore_wait(known.at[3], 2)
+    signal(known.at[4], along_z(2), along_z(-2))
 
     def flip(inner, outer):
         value = zb[outer + 1, pl.ds((inner - outer + 1) * SUP, SUP), :]
@@ -206,8 +269,14 @@
         for row in range(3):
             acc[own, pl.ds(row * SUP, SUP), :] = near(sb, zb.at[own + 1], own, row, local[own])
 
+    pl.semaphore_wait(known.at[1], 1)
+    signal(known.at[2], along_x(1), along_x(-1))
+    pl.semaphore_wait(known.at[4], 2)
+    signal(known.at[5], along_z(4), along_z(-4))
+
     for copy in s_halo:
         copy.wait_recv()
+    mask_halo(sb, 1.0, 1.0)
     for own in (0, 1):
         for row in range(3):
             where = (own, pl.ds(row * SUP, SUP), slice(None))
@@ -230,38 +299,52 @@
 
     squares = jnp.zeros((8, B), jnp.float32)
 
-    def defect(own, row, squares):
-        total = near(zt, pb.at[own], own, row, (0, 1, 2))
-        if row == 0:
-            total = total + dot(tu[own], zb[own + 1, pl.ds(0, SUP), :])
-        if row == 2:
-            total = total + dot(td[own], zb[own + 1, pl.ds(2 * SUP, SUP), :])
+    def defect(own, row, total, squares):
         for r, c, column, offset in blocks_of(own, row):
             block = -total[r * B : (r + 1) * B, c * B : (c + 1) * B]
             if offset == W:
                 block = eye + block
-            block = (block * present(column, offset)).astype(jnp.bfloat16)
+            else:
+                block = block * present(column, offset)
+            block = block.astype(jnp.bfloat16)
             db[own + 1, pl.ds((2 * row + r) * B, B), pl.ds(c * B, B)] = block
             wide = block.astype(jnp.float32)
             squares = squares + jnp.sum((wide * wide).reshape(B // 8, 8, B), axis=0)
         return squares
 
+    def outer(own, row):
+        corner = (tu, td)[row // 2]
+        return dot(corner[own], zb[own + 1, pl.ds(row * SUP, SUP), :])
+
     for own, rows in ((0, (1, 2)), (1, (0, 1))):
         for row in rows:
-            squares = defect(own, row, squares)
-
-    for copy in z_halo + t_halo:
+            total = near(zt, pb.at[own], own, row, (0, 1, 2))
+            if row != 1:
+                total = total + outer(own, row)
+            squares = defect(own, row, total, squares)
+
+    pl.semaphore_wait(known.at[2], 2)
+    signal(known.at[6], along_x(2))
+    pl.semaphore_wait(known.at[5], 2)
+
+    for copy in z_halo:
         copy.wait_recv()
+    mask_halo(zb, first, last)
     flip(-1, -1)
     flip(0, -1)
     flip(1, 2)
     flip(2, 2)
-    squares = defect(0, 0, squares)
-    squares = defect(1, 2, squares)
-
-    d_halo = send_band(db)
+    edges = ((0, 0), (1, 2))
+    for own, row in edges:
+        acc[own, pl.ds(row * SUP, SUP), :] = near(zt, pb.at[own], own, row, (0, 1, 2))
+    for copy in t_halo:
+        copy.wait_recv()
+    for own, row in edges:
+        total = acc[own, pl.ds(row * SUP, SUP), :] + outer(own, row)
+        squares = defect(own, row, total, squares)
 
     part_a[in_plane] = jnp.sum(squares, axis=0, keepdims=True)
+    pl.semaphore_wait(known.at[6], 1)
 
     def sum_copy(buffer, slot, stage, peer):
         return pltpu.make_async_remote_copy(
@@ -285,6 +368,7 @@
         return pltpu.make_async_copy(buffer.at[pl.ds(0, rows)], buffer.at[pl.ds(0, rows)], sem)
 
     lax.fori_loop(1, n_plane, send_plane, 0)
+    d_halo = send_band(db)
 
     for own in (0, 1):
         for row in range(3):
@@ -329,6 +413,10 @@
     all_of(part_b, n_z - 1, sum_send.at[1]).wait()
 
 
+def in_hbm(array):
+    return pltpu.with_memory_space_constraint(array, pltpu.HBM)
+
+
 def solution(mesh):
     n_grp, n_slab = mesh.shape["grp"], mesh.shape["slab"]
     n_plane, n_z = n_grp * PLANE, n_slab // PLANE
@@ -345,8 +433,8 @@
                 jax.ShapeDtypeStruct((1, 1), jnp.float32),
             ),
             in_specs=[
-                pl.BlockSpec(memory_space=pl.ANY),
-                pl.BlockSpec(memory_space=pl.ANY),
+                pl.BlockSpec(memory_space=pltpu.HBM),
+                pl.BlockSpec(memory_space=pltpu.HBM),
                 pl.BlockSpec(memory_space=pltpu.SMEM),
             ],
             out_specs=(
@@ -368,16 +456,19 @@
                 pltpu.VMEM((n_plane, 1, B), jnp.float32),
                 pltpu.VMEM((n_z, 1, B), jnp.float32),
                 pltpu.SemaphoreType.DMA((2 * COLS,)),
-                pltpu.SemaphoreType.DMA((14,)),
-                pltpu.SemaphoreType.DMA((14,)),
+                pltpu.SemaphoreType.DMA((COPIES,)),
+                pltpu.SemaphoreType.DMA((COPIES,)),
                 pltpu.SemaphoreType.DMA((2,)),
                 pltpu.SemaphoreType.DMA((2,)),
+                pltpu.SemaphoreType.REGULAR((7,)),
             ],
-            compiler_params=pltpu.CompilerParams(collective_id=0, has_side_effects=True),
+            compiler_params=pltpu.CompilerParams(
+                collective_id=0, has_side_effects=True, vmem_limit_bytes=24 << 20
+            ),
         )(
-            margin.reshape(COLS, OFFS * B, B),
-            factor.reshape(COLS, OFFS * B, B),
-            pattern,
+            in_hbm(margin.reshape(COLS, OFFS * B, B)),
+            in_hbm(factor.reshape(COLS, OFFS * B, B)),
+            in_hbm(pattern),
         )
         return refined, norm.reshape(())
 

time: 44.1 us -> 39.8 us (0.902)
  Pallas kernels: 39.5 us -> 36.5 us
  local copies, waits for them, and re-layouts: 1.99 us -> 0.84 us
    pallas_call x1, Pallas kernels: 39.5 us -> 36.5 us  [step(): pl.pallas_call(functools.partial(kernel, n_grp, n_slab), out_shape=(jax.S...]
    unnamed x1, local copies, waits for them, and re-layouts: 1.99 us -> 0.84 us
where the time goes in v2:
time: 39.8 us; the launch traced here: 39.7 us
  Pallas kernels  36.5 us (92%)
  between operations  2.33 us (6%)
  local copies, waits for them, and re-layouts  0.84 us (2%)
    pallas_call x1, Pallas kernels, step(): pl.pallas_call(functools.partial(kernel, n_grp, n_slab), out_shape=(jax.S...  36.5 us
    unnamed x1, local copies, waits for them, and re-layouts  0.84 us

profile of v2, /device:TPU:1, one launch (start us, length us, event | category | flops | bytes accessed | tf_op | source)
XLA Modules:
  0.0 39.7 jit_solution(11111947701388409414)
XLA Ops:
  0.6 36.5 %shard_map.50 = (bf16[4,5,128,128]{3,2,1,0:T(8,128)(2,1)S(1)}, f32[1,1]{1,0:T(1,128)}) custom-call(bf16[4,640,128]{2,1,0:T(8,128)(2,1)} %bitcast.3, bf16[4,640,128]{2,1,0:T(8,128)(2,1)} %bitcast.4, s32[4,5]{1,0:T(4,128)} %pat.1), custom_call_target="tpu_custom_call" | custom-call | tf_op jit(solution)/shard_map/pallas_call | solution.py:429
  37.2 0.8 %copy.7 = bf16[4,5,128,128]{3,2,1,0:T(8,128)(2,1)} copy(bf16[4,5,128,128]{3,2,1,0:T(8,128)(2,1)S(1)} %get-tuple-element.8) | data formatting | bytes 1310720

commit v3 on v2

--- a/solution.py
+++ b/solution.py
@@ -14,7 +14,7 @@
 SUP = 2 * B
 BAND = 3 * SUP
 PLANE = 8
-COPIES = 26
+COPIES = 28
 MESH = pl.DeviceIdType.MESH
 
 
@@ -27,7 +27,7 @@
     n_slab,
     margin,
     factor,
-    pat,
+    pattern,
     out,
     norm,
     sb,
@@ -49,6 +49,8 @@
     sum_send,
     sum_recv,
     known,
+    pat,
+    pat_sem,
 ):
     grp = lax.axis_index("grp")
     slab = lax.axis_index("slab")
@@ -65,12 +67,30 @@
     z_here = lax.div(slab, PLANE)
     in_plane = grp * PLANE + lax.rem(slab, PLANE)
 
-    def plane_device(index):
-        return (lax.div(index, PLANE), z_here * PLANE + lax.rem(index, PLANE))
-
-    def z_device(index):
-        return (grp, index * PLANE + lax.rem(slab, PLANE))
-
+    row_here, core = lax.div(lax.rem(slab, PLANE), 2), lax.rem(slab, 2)
+    n_row = PLANE // 2
+
+    def along_x(step):
+        return (lax.rem(grp + n_grp + step, n_grp), slab)
+
+    def along_y(step):
+        return (grp, z_here * PLANE + lax.rem(row_here + n_row + step, n_row) * 2 + core)
+
+    def along_z(step):
+        return (grp, lax.rem(slab + n_slab + step * PLANE, n_slab))
+
+    mate = (grp, slab + 1 - 2 * core)
+
+    def signal(sem, *peers):
+        for peer in peers:
+            pl.semaphore_signal(sem, inc=1, device_id=peer, device_id_type=MESH)
+
+    barrier = pltpu.get_barrier_semaphore()
+    near_by = (left, right, along_y(1), along_y(-1), along_x(1), along_x(-1), along_z(1), along_z(-1))
+    signal(barrier, *near_by)
+
+    pattern_copy = pltpu.make_async_copy(pattern, pat, pat_sem)
+    pattern_copy.start()
     loads = {}
     for which, (source, band) in enumerate(((margin, sb), (factor, zb))):
         for column in range(COLS):
@@ -83,28 +103,6 @@
             copy.start()
             loads[which, column] = copy
 
-    row_here, core = lax.div(lax.rem(slab, PLANE), 2), lax.rem(slab, 2)
-    n_row = PLANE // 2
-
-    def along_x(step):
-        return (lax.rem(grp + n_grp + step, n_grp), slab)
-
-    def along_y(step):
-        return (grp, z_here * PLANE + lax.rem(row_here + n_row + step, n_row) * 2 + core)
-
-    def along_z(step):
-        return (grp, lax.rem(slab + n_slab + step * PLANE, n_slab))
-
-    mate = (grp, slab + 1 - 2 * core)
-
-    def signal(sem, *peers):
-        for peer in peers:
-            pl.semaphore_signal(sem, inc=1, device_id=peer, device_id_type=MESH)
-
-    barrier = pltpu.get_barrier_semaphore()
-    near_by = (left, right, along_y(1), along_y(-1), along_x(1), along_x(-1), along_z(1), along_z(-1))
-    signal(barrier, *near_by)
-
     blank = jnp.zeros((B, B), jnp.bfloat16)
     for band in (sb, zb, db):
         for index in range(4):
@@ -114,11 +112,19 @@
         eb[index, pl.ds(5 * B, B), pl.ds(0, B)] = blank
         eb[index, pl.ds(0, B), pl.ds(B, B)] = blank
 
+    inner_left, inner_right = slab > 0, slab < n_slab - 1
+
+    @pl.when(jnp.logical_not(inner_left))
+    def _():
+        sb[0, pl.ds(SUP, 2 * SUP), :] = jnp.zeros((2 * SUP, SUP), jnp.bfloat16)
+        zb[0, pl.ds(2 * SUP, SUP), :] = jnp.zeros((SUP, SUP), jnp.bfloat16)
+        tu[0] = jnp.zeros((SUP, SUP), jnp.bfloat16)
+
     def present(column, offset):
         return pat[column, offset].astype(jnp.float32)
 
-    first = (slab > 0).astype(jnp.float32)
-    last = (slab < n_slab - 1).astype(jnp.float32)
+    first = inner_left.astype(jnp.float32)
+    last = inner_right.astype(jnp.float32)
 
     def place(index, half, block, blocks=1):
         return (index, pl.ds(block * B, blocks * B), pl.ds(half * B, B))
@@ -129,11 +135,11 @@
 
     pl.semaphore_wait(barrier, len(near_by))
 
-    started = []
-
-    def send(source, target, peer):
-        index = len(started)
-        copy = pltpu.make_async_remote_copy(
+    used = iter(range(COPIES))
+
+    def remote(source, target, peer):
+        index = next(used)
+        return pltpu.make_async_remote_copy(
             src_ref=source,
             dst_ref=target,
             send_sem=send_sem.at[index],
@@ -141,68 +147,71 @@
             device_id=peer,
             device_id_type=MESH,
         )
-        copy.start()
-        started.append(copy)
-        return copy
-
-    def send_band(band):
-        to_left = [
-            send(
-                band.at[1, pl.ds(first_row, rows), pl.ds(half * B, B)],
-                band.at[3, pl.ds(first_row, rows), pl.ds(half * B, B)],
-                left,
+
+    def all_start(copies):
+        for copy in copies:
+            copy.start()
+
+    def all_arrived(copies):
+        for copy in copies:
+            copy.wait_recv()
+
+    def all_sent(copies):
+        for copy in copies:
+            copy.wait_send()
+
+    raw_left, raw_right = ((0, 0, 3), (1, 0, 1), (1, 2, 1)), ((3, 2, 3), (2, 2, 1), (2, 4, 1))
+    raw_edge = ((2, 2, 1), (3, 2, 1))
+    own_left, own_right = ((0, 3), (1, 1)), ((2, 3), (3, 1))
+
+    def raw(source, band, pieces, target, peer):
+        return [
+            remote(
+                source.at[column, pl.ds(offset * B, offsets * B), :],
+                band.at[place(target, column % 2, offset + column % 2, offsets)],
+                peer,
             )
-            for half, first_row, rows in ((0, 0, 4 * B), (1, B, 3 * B))
+            for column, offset, offsets in pieces
         ]
-        to_right = [
-            send(
-                band.at[2, pl.ds(first_row, rows), pl.ds(half * B, B)],
-                band.at[0, pl.ds(first_row, rows), pl.ds(half * B, B)],
-                right,
+
+    def masked(band, pieces, target, peer):
+        return [
+            remote(
+                band.at[place(1 + column // 2, column % 2, offset + column % 2)],
+                band.at[place(target, column % 2, offset + column % 2)],
+                peer,
             )
-            for half, first_row, rows in ((0, 2 * B, 3 * B), (1, 2 * B, 4 * B))
+            for column, offset in pieces
         ]
-        return to_left + to_right
-
-    raw_left, raw_right = ((0, 0, 3), (1, 0, 1), (1, 2, 1)), ((2, 2, 1), (2, 4, 1), (3, 2, 3))
-    own_left, own_right = ((0, 3), (1, 1)), ((2, 3), (3, 1))
-
-    def send_raw(source, band):
-        copies = []
-        for index in range(3):
-            for peer, target, pieces in ((left, 3, raw_left), (right, 0, raw_right)):
-                column, offset, offsets = pieces[index]
-                half = column % 2
-                copies.append(
-                    send(
-                        source.at[column, pl.ds(offset * B, offsets * B), :],
-                        band.at[place(target, half, offset + half, offsets)],
-                        peer,
-                    )
-                )
-        return copies
-
-    def send_own(band):
-        copies = []
-        for index in range(2):
-            for peer, target, pieces in ((left, 3, own_left), (right, 0, own_right)):
-                column, offset = pieces[index]
-                half = column % 2
-                copies.append(
-                    send(
-                        band.at[place(1 + column // 2, half, offset + half)],
-                        band.at[place(target, half, offset + half)],
-                        peer,
-                    )
-                )
-        return copies
-
-    s_halo = send_raw(margin, sb)
-    z_halo = send_raw(factor, zb)
+
+    s_raw_left = raw(margin, sb, raw_left, 3, left)
+    s_raw_right = raw(margin, sb, raw_right, 0, right)
+    z_raw_left = raw(factor, zb, raw_left, 3, left)
+    z_raw_right = raw(factor, zb, raw_right, 0, right)
+    z_raw_edge = raw(factor, zb, raw_edge, 0, right)
+    s_own_left, s_own_right = masked(sb, own_left, 3, left), masked(sb, own_right, 0, right)
+    z_own_left, z_own_right = masked(zb, own_left, 3, left), masked(zb, own_right, 0, right)
+
+    @pl.when(inner_right)
+    def _():
+        all_start(s_raw_right)
+
+    @pl.when(jnp.logical_not(inner_right))
+    def _():
+        all_start(z_raw_edge)
+
+    all_start(s_raw_left)
+
+    @pl.when(inner_right)
+    def _():
+        all_start(z_raw_right)
+
+    all_start(z_raw_left)
     signal(known.at[0], along_y(1), along_y(-1))
     signal(known.at[3], along_z(1), along_z(-1))
-
-    for which, (band, halo_copies) in enumerate(((sb, s_halo), (zb, z_halo))):
+    pattern_copy.wait()
+
+    def mask_own(which, band):
         for column in range(COLS):
             loads[which, column].wait()
         for column in range(COLS):
@@ -217,13 +226,24 @@
                 if which == 1 and row >= COLS:
                     scale = scale * last
                 scale_block(band, place(1 + column // 2, half, half + offset), scale)
-        halo_copies.extend(send_own(band))
-
-    def mask_halo(band, low, high):
+
+    mask_own(0, sb)
+
+    @pl.when(inner_right)
+    def _():
+        all_start(s_own_right)
+
+    all_start(s_own_left)
+    mask_own(1, zb)
+    all_start(z_own_right + z_own_left)
+
+    def mask_low(band):
         for half, block, column, offset in ((0, 4, 0, 0), (1, 4, 0, 1), (1, 5, 1, 0)):
-            scale_block(band, place(0, half, block), present(column, offset) * low)
+            scale_block(band, place(0, half, block), present(column, offset))
+
+    def mask_high(band, scale):
         for half, block, column, offset in ((0, 0, 2, 4), (0, 1, 3, 3), (1, 1, 3, 4)):
-            scale_block(band, place(3, half, block), present(column, offset) * high)
+            scale_block(band, place(3, half, block), present(column, offset) * scale)
 
     pl.semaphore_wait(known.at[0], 2)
     signal(known.at[1], mate)
@@ -246,7 +266,13 @@
 
     ts[0] = lower(0).astype(jnp.bfloat16)
     ts[1] = upper(1).astype(jnp.bfloat16)
-    t_halo = [send(ts.at[0], td.at[1], left), send(ts.at[1], tu.at[0], right)]
+    t_left, t_right = [remote(ts.at[0], td.at[1], left)], [remote(ts.at[1], tu.at[0], right)]
+
+    @pl.when(inner_right)
+    def _():
+        all_start(t_right)
+
+    all_start(t_left)
     tu[1] = upper(0).astype(jnp.bfloat16)
     td[0] = lower(1).astype(jnp.bfloat16)
 
@@ -274,9 +300,13 @@
     pl.semaphore_wait(known.at[4], 2)
     signal(known.at[5], along_z(4), along_z(-4))
 
-    for copy in s_halo:
-        copy.wait_recv()
-    mask_halo(sb, 1.0, 1.0)
+    @pl.when(inner_left)
+    def _():
+        all_arrived(s_raw_right + s_own_right)
+        mask_low(sb)
+
+    all_arrived(s_raw_left + s_own_left)
+    mask_high(sb, 1.0)
     for own in (0, 1):
         for row in range(3):
             where = (own, pl.ds(row * SUP, SUP), slice(None))
@@ -327,9 +357,17 @@
     signal(known.at[6], along_x(2))
     pl.semaphore_wait(known.at[5], 2)
 
-    for copy in z_halo:
-        copy.wait_recv()
-    mask_halo(zb, first, last)
+    @pl.when(inner_left)
+    def _():
+        all_arrived(z_raw_right)
+        mask_low(zb)
+
+    @pl.when(jnp.logical_not(inner_left))
+    def _():
+        all_arrived(z_raw_edge)
+
+    all_arrived(z_own_right + z_raw_left + z_own_left)
+    mask_high(zb, last)
     flip(-1, -1)
     flip(0, -1)
     flip(1, 2)
@@ -337,8 +375,11 @@
     edges = ((0, 0), (1, 2))
     for own, row in edges:
         acc[own, pl.ds(row * SUP, SUP), :] = near(zt, pb.at[own], own, row, (0, 1, 2))
-    for copy in t_halo:
-        copy.wait_recv()
+    @pl.when(inner_left)
+    def _():
+        all_arrived(t_right)
+
+    all_arrived(t_left)
     for own, row in edges:
         total = acc[own, pl.ds(row * SUP, SUP), :] + outer(own, row)
         squares = defect(own, row, total, squares)
@@ -356,19 +397,37 @@
             device_id_type=MESH,
         )
 
-    def send_plane(step, carry):
-        sum_copy(part_a, in_plane, 0, plane_device(lax.rem(in_plane + step, n_plane))).start()
-        return carry
-
-    def send_z(step, carry):
-        sum_copy(part_b, z_here, 1, z_device(lax.rem(z_here + step, n_z))).start()
-        return carry
+    def hops(step, size):
+        return min(step, size - step)
+
+    plane_steps = sorted(
+        ((x, y, c) for x in range(n_grp) for y in range(n_row) for c in range(2) if x or y or c),
+        key=lambda step: -hops(step[0], n_grp) - hops(step[1], n_row),
+    )
+    z_steps = sorted(range(1, n_z), key=lambda step: -hops(step, n_z))
 
     def all_of(buffer, rows, sem):
         return pltpu.make_async_copy(buffer.at[pl.ds(0, rows)], buffer.at[pl.ds(0, rows)], sem)
 
-    lax.fori_loop(1, n_plane, send_plane, 0)
-    d_halo = send_band(db)
+    x_of = [lax.rem(grp + step, n_grp) for step in range(n_grp)]
+    y_of = [z_here * PLANE + 2 * lax.rem(row_here + step, n_row) for step in range(n_row)]
+    core_of = (core, 1 - core)
+    for x, y, c in plane_steps:
+        sum_copy(part_a, in_plane, 0, (x_of[x], y_of[y] + core_of[c])).start()
+    d_halo = [
+        remote(
+            db.at[index, pl.ds(first_row, rows), pl.ds(half * B, B)],
+            db.at[target, pl.ds(first_row, rows), pl.ds(half * B, B)],
+            peer,
+        )
+        for index, target, peer, half, first_row, rows in (
+            (1, 3, left, 0, 0, 4 * B),
+            (2, 0, right, 1, 2 * B, 4 * B),
+            (1, 3, left, 1, B, 3 * B),
+            (2, 0, right, 0, 2 * B, 3 * B),
+        )
+    ]
+    all_start(d_halo)
 
     for own in (0, 1):
         for row in range(3):
@@ -378,10 +437,10 @@
 
     all_of(part_a, n_plane - 1, sum_recv.at[0]).wait()
     part_b[z_here] = jnp.sum(part_a[...], axis=0)
-    lax.fori_loop(1, n_z, send_z, 0)
-
-    for copy in d_halo:
-        copy.wait_recv()
+    for step in z_steps:
+        sum_copy(part_b, z_here, 1, along_z(step)).start()
+
+    all_arrived(d_halo)
     for own in (0, 1):
         for row in range(3):
             total = acc2[own, pl.ds(row * SUP, SUP), :]
@@ -403,14 +462,21 @@
                 block = (block + base.astype(jnp.float32)) * present(column, offset)
                 out[column, offset] = block.astype(jnp.bfloat16)
 
+    @pl.when(inner_right)
+    def _():
+        all_sent(s_raw_right + s_own_right + z_raw_right + t_right)
+
+    @pl.when(jnp.logical_not(inner_right))
+    def _():
+        all_sent(z_raw_edge)
+
+    all_sent(s_raw_left + s_own_left + z_raw_left + z_own_left + z_own_right + t_left + d_halo)
+    all_of(part_a, n_plane - 1, sum_send.at[0]).wait()
+    all_of(part_b, n_z - 1, sum_send.at[1]).wait()
+
     all_of(part_b, n_z - 1, sum_recv.at[1]).wait()
     total = jnp.sum(jnp.sum(part_b[...], axis=0), axis=1, keepdims=True)
     norm[...] = jnp.sqrt(total / (count * COLS * B))
-
-    for copy in started:
-        copy.wait_send()
-    all_of(part_a, n_plane - 1, sum_send.at[0]).wait()
-    all_of(part_b, n_z - 1, sum_send.at[1]).wait()
 
 
 def in_hbm(array):
@@ -435,7 +501,7 @@
             in_specs=[
                 pl.BlockSpec(memory_space=pltpu.HBM),
                 pl.BlockSpec(memory_space=pltpu.HBM),
-                pl.BlockSpec(memory_space=pltpu.SMEM),
+                pl.BlockSpec(memory_space=pltpu.HBM),
             ],
             out_specs=(
                 pl.BlockSpec(memory_space=pltpu.VMEM),
@@ -461,6 +527,8 @@
                 pltpu.SemaphoreType.DMA((2,)),
                 pltpu.SemaphoreType.DMA((2,)),
                 pltpu.SemaphoreType.REGULAR((7,)),
+                pltpu.SMEM((COLS, OFFS), jnp.int32),
+                pltpu.SemaphoreType.DMA,
             ],
             compiler_params=pltpu.CompilerParams(
                 collective_id=0, has_side_effects=True, vmem_limit_bytes=24 << 20

time: 39.8 us -> 38.9 us (0.977)
  Pallas kernels: 36.5 us -> 35.6 us
    pallas_call x1, Pallas kernels: 36.5 us -> 35.6 us  [step(): pl.pallas_call(functools.partial(kernel, n_grp, n_slab), out_shape=(jax.S...]
where the time goes in v3:
time: 38.9 us; the launch traced here: 38.7 us
  Pallas kernels  35.6 us (92%)
  between operations  2.33 us (6%)
  local copies, waits for them, and re-layouts  0.84 us (2%)
    pallas_call x1, Pallas kernels, step(): pl.pallas_call(functools.partial(kernel, n_grp, n_slab), out_shape=(jax.S...  35.6 us
    unnamed x1, local copies, waits for them, and re-layouts  0.84 us

profile of v3, /device:TPU:1, one launch (start us, length us, event | category | flops | bytes accessed | tf_op | source)
XLA Modules:
  0.0 38.7 jit_solution(2318799055189799095)
XLA Ops:
  0.6 35.6 %shard_map.50 = (bf16[4,5,128,128]{3,2,1,0:T(8,128)(2,1)S(1)}, f32[1,1]{1,0:T(1,128)}) custom-call(bf16[4,640,128]{2,1,0:T(8,128)(2,1)} %bitcast.3, bf16[4,640,128]{2,1,0:T(8,128)(2,1)} %bitcast.4, s32[4,5]{1,0:T(4,128)} %pattern.1), custom_call_target="tpu_custom_call" | custom-call | tf_op jit(solution)/shard_map/pallas_call | solution.py:495
  36.2 0.8 %copy.7 = bf16[4,5,128,128]{3,2,1,0:T(8,128)(2,1)} copy(bf16[4,5,128,128]{3,2,1,0:T(8,128)(2,1)S(1)} %get-tuple-element.8) | data formatting | bytes 1310720

commit v4 on v3

--- a/solution.py
+++ b/solution.py
@@ -14,7 +14,7 @@
 SUP = 2 * B
 BAND = 3 * SUP
 PLANE = 8
-COPIES = 28
+COPIES = 30
 MESH = pl.DeviceIdType.MESH
 
 
@@ -120,6 +120,12 @@
         zb[0, pl.ds(2 * SUP, SUP), :] = jnp.zeros((SUP, SUP), jnp.bfloat16)
         tu[0] = jnp.zeros((SUP, SUP), jnp.bfloat16)
 
+    @pl.when(jnp.logical_not(inner_right))
+    def _():
+        sb[3, pl.ds(0, 2 * SUP), :] = jnp.zeros((2 * SUP, SUP), jnp.bfloat16)
+        zb[3, pl.ds(0, SUP), :] = jnp.zeros((SUP, SUP), jnp.bfloat16)
+        td[1] = jnp.zeros((SUP, SUP), jnp.bfloat16)
+
     def present(column, offset):
         return pat[column, offset].astype(jnp.float32)
 
@@ -161,7 +167,7 @@
             copy.wait_send()
 
     raw_left, raw_right = ((0, 0, 3), (1, 0, 1), (1, 2, 1)), ((3, 2, 3), (2, 2, 1), (2, 4, 1))
-    raw_edge = ((2, 2, 1), (3, 2, 1))
+    edge_left, edge_right = ((0, 2, 1), (1, 2, 1)), ((2, 2, 1), (3, 2, 1))
     own_left, own_right = ((0, 3), (1, 1)), ((2, 3), (3, 1))
 
     def raw(source, band, pieces, target, peer):
@@ -188,7 +194,8 @@
     s_raw_right = raw(margin, sb, raw_right, 0, right)
     z_raw_left = raw(factor, zb, raw_left, 3, left)
     z_raw_right = raw(factor, zb, raw_right, 0, right)
-    z_raw_edge = raw(factor, zb, raw_edge, 0, right)
+    z_edge_left = raw(factor, zb, edge_left, 3, left)
+    z_edge_right = raw(factor, zb, edge_right, 0, right)
     s_own_left, s_own_right = masked(sb, own_left, 3, left), masked(sb, own_right, 0, right)
     z_own_left, z_own_right = masked(zb, own_left, 3, left), masked(zb, own_right, 0, right)
 
@@ -196,17 +203,26 @@
     def _():
         all_start(s_raw_right)
 
+    @pl.when(inner_left)
+    def _():
+        all_start(s_raw_left)
+
+    @pl.when(inner_right)
+    def _():
+        all_start(z_raw_right)
+
     @pl.when(jnp.logical_not(inner_right))
     def _():
-        all_start(z_raw_edge)
-
-    all_start(s_raw_left)
-
-    @pl.when(inner_right)
-    def _():
-        all_start(z_raw_right)
-
-    all_start(z_raw_left)
+        all_start(z_edge_right)
+
+    @pl.when(inner_left)
+    def _():
+        all_start(z_raw_left)
+
+    @pl.when(jnp.logical_not(inner_left))
+    def _():
+        all_start(z_edge_left)
+
     signal(known.at[0], along_y(1), along_y(-1))
     signal(known.at[3], along_z(1), along_z(-1))
     pattern_copy.wait()
@@ -233,7 +249,10 @@
     def _():
         all_start(s_own_right)
 
-    all_start(s_own_left)
+    @pl.when(inner_left)
+    def _():
+        all_start(s_own_left)
+
     mask_own(1, zb)
     all_start(z_own_right + z_own_left)
 
@@ -241,9 +260,9 @@
         for half, block, column, offset in ((0, 4, 0, 0), (1, 4, 0, 1), (1, 5, 1, 0)):
             scale_block(band, place(0, half, block), present(column, offset))
 
-    def mask_high(band, scale):
+    def mask_high(band):
         for half, block, column, offset in ((0, 0, 2, 4), (0, 1, 3, 3), (1, 1, 3, 4)):
-            scale_block(band, place(3, half, block), present(column, offset) * scale)
+            scale_block(band, place(3, half, block), present(column, offset))
 
     pl.semaphore_wait(known.at[0], 2)
     signal(known.at[1], mate)
@@ -272,7 +291,10 @@
     def _():
         all_start(t_right)
 
-    all_start(t_left)
+    @pl.when(inner_left)
+    def _():
+        all_start(t_left)
+
     tu[1] = upper(0).astype(jnp.bfloat16)
     td[0] = lower(1).astype(jnp.bfloat16)
 
@@ -305,8 +327,11 @@
         all_arrived(s_raw_right + s_own_right)
         mask_low(sb)
 
-    all_arrived(s_raw_left + s_own_left)
-    mask_high(sb, 1.0)
+    @pl.when(inner_right)
+    def _():
+        all_arrived(s_raw_left + s_own_left)
+        mask_high(sb)
+
     for own in (0, 1):
         for row in range(3):
             where = (own, pl.ds(row * SUP, SUP), slice(None))
@@ -364,10 +389,18 @@
 
     @pl.when(jnp.logical_not(inner_left))
     def _():
-        all_arrived(z_raw_edge)
-
-    all_arrived(z_own_right + z_raw_left + z_own_left)
-    mask_high(zb, last)
+        all_arrived(z_edge_right)
+
+    @pl.when(inner_right)
+    def _():
+        all_arrived(z_raw_left)
+        mask_high(zb)
+
+    @pl.when(jnp.logical_not(inner_right))
+    def _():
+        all_arrived(z_edge_left)
+
+    all_arrived(z_own_right + z_own_left)
     flip(-1, -1)
     flip(0, -1)
     flip(1, 2)
@@ -379,7 +412,10 @@
     def _():
         all_arrived(t_right)
 
-    all_arrived(t_left)
+    @pl.when(inner_right)
+    def _():
+        all_arrived(t_left)
+
     for own, row in edges:
         total = acc[own, pl.ds(row * SUP, SUP), :] + outer(own, row)
         squares = defect(own, row, total, squares)
@@ -468,15 +504,23 @@
 
     @pl.when(jnp.logical_not(inner_right))
     def _():
-        all_sent(z_raw_edge)
-
-    all_sent(s_raw_left + s_own_left + z_raw_left + z_own_left + z_own_right + t_left + d_halo)
+        all_sent(z_edge_right)
+
+    @pl.when(inner_left)
+    def _():
+        all_sent(s_raw_left + s_own_left + z_raw_left + t_left)
+
+    @pl.when(jnp.logical_not(inner_left))
+    def _():
+        all_sent(z_edge_left)
+
+    all_sent(z_own_left + z_own_right + d_halo)
     all_of(part_a, n_plane - 1, sum_send.at[0]).wait()
     all_of(part_b, n_z - 1, sum_send.at[1]).wait()
 
     all_of(part_b, n_z - 1, sum_recv.at[1]).wait()
     total = jnp.sum(jnp.sum(part_b[...], axis=0), axis=1, keepdims=True)
-    norm[...] = jnp.sqrt(total / (count * COLS * B))
+    norm[...] = jnp.broadcast_to(jnp.sqrt(total / (count * COLS * B)), (8, B))
 
 
 def in_hbm(array):
@@ -496,7 +540,7 @@
             functools.partial(kernel, n_grp, n_slab),
             out_shape=(
                 jax.ShapeDtypeStruct((COLS, OFFS, B, B), jnp.bfloat16),
-                jax.ShapeDtypeStruct((1, 1), jnp.float32),
+                jax.ShapeDtypeStruct((8, B), jnp.float32),
             ),
             in_specs=[
                 pl.BlockSpec(memory_space=pltpu.HBM),
@@ -538,7 +582,7 @@
             in_hbm(factor.reshape(COLS, OFFS * B, B)),
             in_hbm(pattern),
         )
-        return refined, norm.reshape(())
+        return refined, norm[0, 0]
 
     return jax.shard_map(
         step,

time: 38.9 us -> 37.2 us (0.956)
  between operations: 2.33 us -> 0.64 us
  local copies, waits for them, and re-layouts: 0.84 us -> 1.35 us
  Pallas kernels: 35.6 us -> 35.1 us
    slice x0 -> x1, local copies, waits for them, and re-layouts: none -> 0.51 us  [step(): return (refined, norm[0, 0])]
    pallas_call x1, Pallas kernels: 35.6 us -> 35.1 us  [step(): pl.pallas_call(functools.partial(kernel, n_grp, n_slab), out_shape=(jax.S...]
where the time goes in v4:
time: 37.2 us; the launch traced here: 37.1 us
  Pallas kernels  35.1 us (94%)
  local copies, waits for them, and re-layouts  1.35 us (4%)
  between operations  0.64 us (2%)
    pallas_call x1, Pallas kernels, step(): pl.pallas_call(functools.partial(kernel, n_grp, n_slab), out_shape=(jax.S...  35.1 us
    unnamed x1, local copies, waits for them, and re-layouts  0.84 us

profile of v4, /device:TPU:1, one launch (start us, length us, event | category | flops | bytes accessed | tf_op | source)
XLA Modules:
  0.0 37.1 jit_solution(17898257985663364851)
XLA Ops:
  0.6 35.1 %shard_map.50 = (bf16[4,5,128,128]{3,2,1,0:T(8,128)(2,1)S(1)}, f32[8,128]{1,0:T(8,128)S(1)}) custom-call(bf16[4,640,128]{2,1,0:T(8,128)(2,1)} %bitcast.3, bf16[4,640,128]{2,1,0:T(8,128)(2,1)} %bitcast.4, s32[4,5]{1,0:T(4,128)} %pattern.1), custom_call_target="tpu_custom_call" | custom-call | tf_op jit(solution)/shard_map/pallas_call | solution.py:539
  35.7 0.5 %slice.3 = f32[1,1]{1,0:T(1,128)} slice(f32[8,128]{1,0:T(8,128)S(1)} %get-tuple-element.5), slice={[0:1], [0:1]} | slice | bytes 8 | tf_op jit(solution)/shard_map/slice | solution.py:585
  36.2 0.8 %copy.6 = bf16[4,5,128,128]{3,2,1,0:T(8,128)(2,1)} copy(bf16[4,5,128,128]{3,2,1,0:T(8,128)(2,1)S(1)} %get-tuple-element.8) | data formatting | bytes 1310720

commit v5 on v4

--- a/solution.py
+++ b/solution.py
@@ -199,13 +199,21 @@
     s_own_left, s_own_right = masked(sb, own_left, 3, left), masked(sb, own_right, 0, right)
     z_own_left, z_own_right = masked(zb, own_left, 3, left), masked(zb, own_right, 0, right)
 
+    @pl.when(inner_left)
+    def _():
+        all_start(s_raw_left)
+
     @pl.when(inner_right)
     def _():
         all_start(s_raw_right)
 
     @pl.when(inner_left)
     def _():
-        all_start(s_raw_left)
+        all_start(z_raw_left)
+
+    @pl.when(jnp.logical_not(inner_left))
+    def _():
+        all_start(z_edge_left)
 
     @pl.when(inner_right)
     def _():
@@ -214,14 +222,6 @@
     @pl.when(jnp.logical_not(inner_right))
     def _():
         all_start(z_edge_right)
-
-    @pl.when(inner_left)
-    def _():
-        all_start(z_raw_left)
-
-    @pl.when(jnp.logical_not(inner_left))
-    def _():
-        all_start(z_edge_left)
 
     signal(known.at[0], along_y(1), along_y(-1))
     signal(known.at[3], along_z(1), along_z(-1))
@@ -245,16 +245,16 @@
 
     mask_own(0, sb)
 
+    @pl.when(inner_left)
+    def _():
+        all_start(s_own_left)
+
     @pl.when(inner_right)
     def _():
         all_start(s_own_right)
 
-    @pl.when(inner_left)
-    def _():
-        all_start(s_own_left)
-
     mask_own(1, zb)
-    all_start(z_own_right + z_own_left)
+    all_start(z_own_left + z_own_right)
 
     def mask_low(band):
         for half, block, column, offset in ((0, 4, 0, 0), (1, 4, 0, 1), (1, 5, 1, 0)):
@@ -283,17 +283,18 @@
     def lower(column):
         return dot(zt[column + 2, pl.ds(0, SUP), :], sb[column + 1, pl.ds(2 * SUP, SUP), :])
 
+    t_left, t_right = [remote(ts.at[0], td.at[1], left)], [remote(ts.at[1], tu.at[0], right)]
     ts[0] = lower(0).astype(jnp.bfloat16)
+
+    @pl.when(inner_left)
+    def _():
+        all_start(t_left)
+
     ts[1] = upper(1).astype(jnp.bfloat16)
-    t_left, t_right = [remote(ts.at[0], td.at[1], left)], [remote(ts.at[1], tu.at[0], right)]
 
     @pl.when(inner_right)
     def _():
         all_start(t_right)
-
-    @pl.when(inner_left)
-    def _():
-        all_start(t_left)
 
     tu[1] = upper(0).astype(jnp.bfloat16)
     td[0] = lower(1).astype(jnp.bfloat16)
@@ -521,6 +522,19 @@
     all_of(part_b, n_z - 1, sum_recv.at[1]).wait()
     total = jnp.sum(jnp.sum(part_b[...], axis=0), axis=1, keepdims=True)
     norm[...] = jnp.broadcast_to(jnp.sqrt(total / (count * COLS * B)), (8, B))
+
+
+def finish(refined, norm, refined_out, norm_out, cell, sem):
+    cell[...] = norm[0:1, 0:1]
+    copies = [pltpu.make_async_copy(cell, norm_out, sem.at[COLS])]
+    for column in range(COLS):
+        copies.append(
+            pltpu.make_async_copy(refined.at[column], refined_out.at[column], sem.at[column])
+        )
+    for copy in copies:
+        copy.start()
+    for copy in copies:
+        copy.wait()
 
 
 def in_hbm(array):
@@ -582,7 +596,21 @@
             in_hbm(factor.reshape(COLS, OFFS * B, B)),
             in_hbm(pattern),
         )
-        return refined, norm[0, 0]
+        refined, norm = pl.pallas_call(
+            finish,
+            out_shape=(
+                jax.ShapeDtypeStruct((COLS, OFFS, B, B), jnp.bfloat16),
+                jax.ShapeDtypeStruct((1, 1), jnp.float32),
+            ),
+            in_specs=[pl.BlockSpec(memory_space=pltpu.VMEM)] * 2,
+            out_specs=(pl.BlockSpec(memory_space=pl.ANY), pl.BlockSpec(memory_space=pl.ANY)),
+            scratch_shapes=[
+                pltpu.VMEM((1, 1), jnp.float32),
+                pltpu.SemaphoreType.DMA((COLS + 1,)),
+            ],
+            compiler_params=pltpu.CompilerParams(vmem_limit_bytes=8 << 20),
+        )(refined, norm)
+        return refined, norm.reshape(())
 
     return jax.shard_map(
         step,

time: 37.2 us -> 36.7 us (0.987)
  local copies, waits for them, and re-layouts: 1.35 us -> 0 us
  Pallas kernels: 35.1 us -> 36 us
    pallas_call x0 -> x1, Pallas kernels: none -> 0.88 us  [step(): pl.pallas_call(finish, out_shape=(jax.ShapeDtypeStruct((COLS, OFFS, B, B)...]
    unnamed x1 -> x0, local copies, waits for them, and re-layouts: 0.84 us -> none
    slice x1 -> x0, local copies, waits for them, and re-layouts: 0.51 us -> none  [step(): return (refined, norm[0, 0])]
where the time goes in v5:
time: 36.7 us; the launch traced here: 36.6 us
  Pallas kernels  36 us (98%)
  between operations  0.64 us (2%)
    pallas_call x1, Pallas kernels, step(): pl.pallas_call(functools.partial(kernel, n_grp, n_slab), out_shape=(jax.S...  35.1 us
    pallas_call x1, Pallas kernels, step(): pl.pallas_call(finish, out_shape=(jax.ShapeDtypeStruct((COLS, OFFS, B, B)...  0.88 us

profile of v5, /device:TPU:1, one launch (start us, length us, event | category | flops | bytes accessed | tf_op | source)
XLA Modules:
  0.0 36.6 jit_solution(16420057103065427026)
XLA Ops:
  0.6 35.1 %shard_map.50 = (bf16[4,5,128,128]{3,2,1,0:T(8,128)(2,1)S(1)}, f32[8,128]{1,0:T(8,128)S(1)}) custom-call(bf16[4,640,128]{2,1,0:T(8,128)(2,1)} %bitcast.3, bf16[4,640,128]{2,1,0:T(8,128)(2,1)} %bitcast.4, s32[4,5]{1,0:T(4,128)} %pattern.1), custom_call_target="tpu_custom_call" | custom-call | tf_op jit(solution)/shard_map/pallas_call | solution.py:553
  35.7 0.9 %shard_map.51 = (bf16[4,5,128,128]{3,2,1,0:T(8,128)(2,1)}, f32[1,1]{1,0:T(1,128)}) custom-call(bf16[4,5,128,128]{3,2,1,0:T(8,128)(2,1)S(1)} %get-tuple-element.6.refined, f32[8,128]{1,0:T(8,128)S(1)} %get-tuple-element.7.norm), custom_call_target="tpu_custom_call" | custom-call | tf_op jit(solution)/shard_map/pallas_call | solution.py:599

commit v6 on v5

--- a/solution.py
+++ b/solution.py
@@ -14,7 +14,7 @@
 SUP = 2 * B
 BAND = 3 * SUP
 PLANE = 8
-COPIES = 30
+COPIES = 18
 MESH = pl.DeviceIdType.MESH
 
 
@@ -139,8 +139,6 @@
         factors = jnp.full((B, B), scale, jnp.float32).astype(jnp.bfloat16)
         band[where] = band[where] * factors
 
-    pl.semaphore_wait(barrier, len(near_by))
-
     used = iter(range(COPIES))
 
     def remote(source, target, peer):
@@ -166,66 +164,23 @@
         for copy in copies:
             copy.wait_send()
 
-    raw_left, raw_right = ((0, 0, 3), (1, 0, 1), (1, 2, 1)), ((3, 2, 3), (2, 2, 1), (2, 4, 1))
-    edge_left, edge_right = ((0, 2, 1), (1, 2, 1)), ((2, 2, 1), (3, 2, 1))
-    own_left, own_right = ((0, 3), (1, 1)), ((2, 3), (3, 1))
-
-    def raw(source, band, pieces, target, peer):
+    pieces_left, pieces_right = ((0, 0, 4), (1, 0, 3)), ((2, 2, 3), (3, 1, 4))
+    edge_left, edge_right = ((0, 2, 2), (1, 1, 2)), ((2, 2, 2), (3, 1, 2))
+
+    def halo_copies(band, pieces, target, peer):
         return [
             remote(
-                source.at[column, pl.ds(offset * B, offsets * B), :],
+                band.at[place(1 + column // 2, column % 2, offset + column % 2, offsets)],
                 band.at[place(target, column % 2, offset + column % 2, offsets)],
                 peer,
             )
             for column, offset, offsets in pieces
         ]
 
-    def masked(band, pieces, target, peer):
-        return [
-            remote(
-                band.at[place(1 + column // 2, column % 2, offset + column % 2)],
-                band.at[place(target, column % 2, offset + column % 2)],
-                peer,
-            )
-            for column, offset in pieces
-        ]
-
-    s_raw_left = raw(margin, sb, raw_left, 3, left)
-    s_raw_right = raw(margin, sb, raw_right, 0, right)
-    z_raw_left = raw(factor, zb, raw_left, 3, left)
-    z_raw_right = raw(factor, zb, raw_right, 0, right)
-    z_edge_left = raw(factor, zb, edge_left, 3, left)
-    z_edge_right = raw(factor, zb, edge_right, 0, right)
-    s_own_left, s_own_right = masked(sb, own_left, 3, left), masked(sb, own_right, 0, right)
-    z_own_left, z_own_right = masked(zb, own_left, 3, left), masked(zb, own_right, 0, right)
-
-    @pl.when(inner_left)
-    def _():
-        all_start(s_raw_left)
-
-    @pl.when(inner_right)
-    def _():
-        all_start(s_raw_right)
-
-    @pl.when(inner_left)
-    def _():
-        all_start(z_raw_left)
-
-    @pl.when(jnp.logical_not(inner_left))
-    def _():
-        all_start(z_edge_left)
-
-    @pl.when(inner_right)
-    def _():
-        all_start(z_raw_right)
-
-    @pl.when(jnp.logical_not(inner_right))
-    def _():
-        all_start(z_edge_right)
-
-    signal(known.at[0], along_y(1), along_y(-1))
-    signal(known.at[3], along_z(1), along_z(-1))
-    pattern_copy.wait()
+    s_left, s_right = halo_copies(sb, pieces_left, 3, left), halo_copies(sb, pieces_right, 0, right)
+    z_left, z_right = halo_copies(zb, pieces_left, 3, left), halo_copies(zb, pieces_right, 0, right)
+    z_edge_left = halo_copies(zb, edge_left, 3, left)
+    z_edge_right = halo_copies(zb, edge_right, 0, right)
 
     def mask_own(which, band):
         for column in range(COLS):
@@ -243,26 +198,37 @@
                     scale = scale * last
                 scale_block(band, place(1 + column // 2, half, half + offset), scale)
 
+    pattern_copy.wait()
     mask_own(0, sb)
-
-    @pl.when(inner_left)
-    def _():
-        all_start(s_own_left)
-
-    @pl.when(inner_right)
-    def _():
-        all_start(s_own_right)
-
+    pl.semaphore_wait(barrier, len(near_by))
+
+    @pl.when(inner_left)
+    def _():
+        all_start(s_left)
+
+    @pl.when(inner_right)
+    def _():
+        all_start(s_right)
+
+    signal(known.at[0], along_y(1), along_y(-1))
+    signal(known.at[3], along_z(1), along_z(-1))
     mask_own(1, zb)
-    all_start(z_own_left + z_own_right)
-
-    def mask_low(band):
-        for half, block, column, offset in ((0, 4, 0, 0), (1, 4, 0, 1), (1, 5, 1, 0)):
-            scale_block(band, place(0, half, block), present(column, offset))
-
-    def mask_high(band):
-        for half, block, column, offset in ((0, 0, 2, 4), (0, 1, 3, 3), (1, 1, 3, 4)):
-            scale_block(band, place(3, half, block), present(column, offset))
+
+    @pl.when(inner_left)
+    def _():
+        all_start(z_left)
+
+    @pl.when(jnp.logical_not(inner_left))
+    def _():
+        all_start(z_edge_left)
+
+    @pl.when(inner_right)
+    def _():
+        all_start(z_right)
+
+    @pl.when(jnp.logical_not(inner_right))
+    def _():
+        all_start(z_edge_right)
 
     pl.semaphore_wait(known.at[0], 2)
     signal(known.at[1], mate)
@@ -325,13 +291,11 @@
 
     @pl.when(inner_left)
     def _():
-        all_arrived(s_raw_right + s_own_right)
-        mask_low(sb)
-
-    @pl.when(inner_right)
-    def _():
-        all_arrived(s_raw_left + s_own_left)
-        mask_high(sb)
+        all_arrived(s_right)
+
+    @pl.when(inner_right)
+    def _():
+        all_arrived(s_left)
 
     for own in (0, 1):
         for row in range(3):
@@ -385,8 +349,7 @@
 
     @pl.when(inner_left)
     def _():
-        all_arrived(z_raw_right)
-        mask_low(zb)
+        all_arrived(z_right)
 
     @pl.when(jnp.logical_not(inner_left))
     def _():
@@ -394,14 +357,12 @@
 
     @pl.when(inner_right)
     def _():
-        all_arrived(z_raw_left)
-        mask_high(zb)
+        all_arrived(z_left)
 
     @pl.when(jnp.logical_not(inner_right))
     def _():
         all_arrived(z_edge_left)
 
-    all_arrived(z_own_right + z_own_left)
     flip(-1, -1)
     flip(0, -1)
     flip(1, 2)
@@ -501,7 +462,7 @@
 
     @pl.when(inner_right)
     def _():
-        all_sent(s_raw_right + s_own_right + z_raw_right + t_right)
+        all_sent(s_right + z_right + t_right)
 
     @pl.when(jnp.logical_not(inner_right))
     def _():
@@ -509,13 +470,13 @@
 
     @pl.when(inner_left)
     def _():
-        all_sent(s_raw_left + s_own_left + z_raw_left + t_left)
+        all_sent(s_left + z_left + t_left)
 
     @pl.when(jnp.logical_not(inner_left))
     def _():
         all_sent(z_edge_left)
 
-    all_sent(z_own_left + z_own_right + d_halo)
+    all_sent(d_halo)
     all_of(part_a, n_plane - 1, sum_send.at[0]).wait()
     all_of(part_b, n_z - 1, sum_send.at[1]).wait()
 

time: 36.7 us -> 36.4 us (level)
  Pallas kernels: 36 us -> 35.6 us
where the time goes in v6:
time: 36.4 us; the launch traced here: 36.3 us
  Pallas kernels  35.6 us (98%)
  between operations  0.64 us (2%)
    pallas_call x1, Pallas kernels, step(): pl.pallas_call(functools.partial(kernel, n_grp, n_slab), out_shape=(jax.S...  34.8 us
    pallas_call x1, Pallas kernels, step(): pl.pallas_call(finish, out_shape=(jax.ShapeDtypeStruct((COLS, OFFS, B, B)...  0.88 us

profile of v6, /device:TPU:1, one launch (start us, length us, event | category | flops | bytes accessed | tf_op | source)
XLA Modules:
  0.0 36.3 jit_solution(1532650728972423376)
XLA Ops:
  0.6 34.8 %shard_map.50 = (bf16[4,5,128,128]{3,2,1,0:T(8,128)(2,1)S(1)}, f32[8,128]{1,0:T(8,128)S(1)}) custom-call(bf16[4,640,128]{2,1,0:T(8,128)(2,1)} %bitcast.3, bf16[4,640,128]{2,1,0:T(8,128)(2,1)} %bitcast.4, s32[4,5]{1,0:T(4,128)} %pattern.1), custom_call_target="tpu_custom_call" | custom-call | tf_op jit(solution)/shard_map/pallas_call | solution.py:514
  35.4 0.9 %shard_map.51 = (bf16[4,5,128,128]{3,2,1,0:T(8,128)(2,1)}, f32[1,1]{1,0:T(1,128)}) custom-call(bf16[4,5,128,128]{3,2,1,0:T(8,128)(2,1)S(1)} %get-tuple-element.6.refined, f32[8,128]{1,0:T(8,128)S(1)} %get-tuple-element.7.norm), custom_call_target="tpu_custom_call" | custom-call | tf_op jit(solution)/shard_map/pallas_call | solution.py:560
